TPU v7x, 256 devices: a whole 4x4x8 slice. The times are simulated.
256 devices in a mesh: samp: 64 (over z, y, core), var: 4 (over x).
Axes of the slice: x: 4, y: 4, z: 8, core: 2. Of those that a mesh axis runs over, the one named last changes fastest.
Arguments:
- dosage: bfloat16 [16384, 40960], P('samp', 'var'), may hold values from 0 to 2
- centers: float32 [40960], replicated, may hold values from 0.4 to 1.34
- scales: float32 [40960], replicated, may hold values from 1.6 to 2.2
- phenotype: float32 [16384], P('samp'), may hold values from -6 to 6
- fold_ids: int32 [16384], P('samp'), may hold values from 0 to 3
- strong_blocks: int32 [32], replicated, may hold values from 0 to 319, as said below
- warm_start: float32 [4096, 32], replicated, may hold values from -4 to 4
- penalty: float32 [8], replicated, may hold values from 0.05 to 0.5
- step_size: float32 [32], replicated, may hold values from 0.2 to 0.6
Outputs:
- margin: float32 [40960], P('var')
- coefficients: float32 [4096, 32], P('var')
Inputs may be any that keep to these rules, and one draw needn't show every extreme that they name: `strong_blocks`: 32 different block numbers.
All inputs are finite; a program needn't handle non-finite values.
Results may differ from a plain program's by a relative error of at most 0.0075.
Values may be sent and summed in bfloat16 or wider, within the bound.
No kernel may reach another device: no remote copies, remote signals or barrier semaphores. Data moves between devices by JAX's collectives and lax.ppermute only.
A program may use at most 64 MiB of HBM per device.

v0:
```python
import math
import jax
import jax.numpy as jnp
from jax import lax
from jax.sharding import PartitionSpec as P

BLOCK = 128
NS = 4096
LAMBDAS = 8
FOLDS = 4
ITERS = 3
exact_mode = lax.Precision.HIGHEST


def shards(
    dosage, centers, scales, phenotype, fold_ids, strong_blocks, warm_start, penalty, step_size
):
    rows, local_width = dosage.shape
    groups = lax.axis_size("var")
    place = lax.axis_index("var")
    fit_total = LAMBDAS * FOLDS
    fit_folds = jnp.arange(fit_total, dtype=jnp.int32) % FOLDS
    weights = (fold_ids[:, None] != fit_folds[None, :]).astype(jnp.float32)
    counts = lax.psum(jnp.sum(weights, axis=0), "samp")
    fit_penalty = jnp.repeat(penalty, FOLDS)
    threshold = step_size * fit_penalty
    local_blocks = local_width // BLOCK
    relative = strong_blocks - place * local_blocks
    owned = (relative >= 0) & (relative < local_blocks)
    picked = jnp.take(
        dosage.reshape(rows, local_blocks, BLOCK), jnp.clip(relative, 0, local_blocks - 1), axis=1
    )
    masked = (picked * owned.astype(jnp.bfloat16)[None, :, None]).reshape(rows, NS)
    columns = (
        strong_blocks[:, None] * BLOCK + jnp.arange(BLOCK, dtype=jnp.int32)[None, :]
    ).reshape(NS)
    strong_centers = centers[columns]
    strong_scales = scales[columns]
    owned_columns = jnp.repeat(owned.astype(jnp.float32), BLOCK)
    share = NS // groups
    point = warm_start
    part_centers = strong_centers * owned_columns
    part_threshold = threshold[None, :]

    def residual_of(coef):
        scaled = (strong_scales[:, None] * coef).astype(jnp.bfloat16)
        partial_fit = jnp.dot(masked, scaled, preferred_element_type=jnp.float32)
        partial_fit = (
            partial_fit - jnp.dot(part_centers * strong_scales, coef, precision=exact_mode)[None, :]
        )
        fitted = lax.psum(partial_fit.astype(jnp.bfloat16), "var").astype(jnp.float32)
        return (weights * (phenotype[:, None] - fitted)).astype(jnp.bfloat16)

    rounded = residual_of(point)
    column_sums = jnp.sum(rounded.astype(jnp.float32), axis=0)
    local_centers = lax.dynamic_slice_in_dim(centers, place * local_width, local_width, 0)
    local_scales = lax.dynamic_slice_in_dim(scales, place * local_width, local_width, 0)
    cross = lax.dot_general(
        dosage, rounded, (((0,), (0,)), ((), ())), preferred_element_type=jnp.float32
    )
    total = lax.psum(cross - local_centers[:, None] * column_sums[None, :], "samp")
    margin = jnp.max(
        jnp.abs(local_scales[:, None] * total / counts[None, :]) / fit_penalty[None, :], axis=1
    )
    momentum = 1.0
    previous = point
    for sweep in range(ITERS):
        if sweep > 0:
            rounded = residual_of(point)
            column_sums = jnp.sum(rounded.astype(jnp.float32), axis=0)
        gradient_cross = lax.dot_general(
            masked, rounded, (((0,), (0,)), ((), ())), preferred_element_type=jnp.float32
        )
        gradient_cross = gradient_cross - part_centers[:, None] * column_sums[None, :]
        gradient_total = lax.psum(gradient_cross, ("samp", "var"))
        moved = point + step_size[None, :] * (
            strong_scales[:, None] * gradient_total / counts[None, :]
        )
        current = moved - jnp.clip(moved, -part_threshold, part_threshold)
        following = (1.0 + math.sqrt(1.0 + 4.0 * momentum * momentum)) / 2.0
        point = current + (momentum - 1.0) / following * (current - previous)
        previous = current
        momentum = following
    coefficients = lax.dynamic_slice_in_dim(previous, place * share, share, 0)
    return (margin, coefficients)


def solution(mesh):
    return jax.shard_map(
        shards,
        mesh=mesh,
        in_specs=(P("samp", "var"), P(), P(), P("samp"), P("samp"), P(), P(), P(), P()),
        out_specs=(P("var"), P("var", None)),
        check_vma=False,
    )
```

profile of v0, /device:TPU:2, one launch (start us, length us, event | category | flops | bytes accessed | tf_op | source)
XLA Modules:
  0.0 1087.9 jit_solution(17105678928884932665)
XLA Ops:
  7.2 0.0 all-reduce.7.cloned.1.call-start
  7.2 7.9 copy.11
  15.2 7.9 copy.12
  23.1 3.4 gather_fusion
  26.6 2.9 copy.13
  29.5 0.1 broadcast_bitcast_fusion
  29.6 0.1 broadcast_bitcast_fusion.1
  29.7 0.1 iota_add_fusion
  29.8 23.0 %gather_fusion.1 = f32[4096]{0:T(1024)S(1)} fusion(f32[40960]{0:T(1024)S(1)} %copy-done.1, s32[4096]{0:T(1024)S(1)} %broadcast_clamp_fusion), kind=kCustom, calls=%fused_computation.1 | custom fusion | bytes 49152 | tf_op jit(solution)/shard_map/gather | solution.py:38
  52.9 23.0 %gather_fusion.2 = f32[4096]{0:T(1024)S(1)} fusion(f32[40960]{0:T(1024)S(1)} %copy-done, s32[4096]{0:T(1024)S(1)} %broadcast_clamp_fusion), kind=kCustom, calls=%fused_computation.2 | custom fusion | bytes 49152 | tf_op jit(solution)/shard_map/gather | solution.py:37
  75.9 0.1 fusion.23
  76.0 0.5 convolution_bitcast_fusion.3
  76.5 3.2 fusion.1
  79.7 0.4 fusion.3
  80.2 15.3 %psum.56 = bf16[256,32]{0,1:T(8,128)(2,1)S(1)} all-reduce(bf16[256,32]{0,1:T(8,128)(2,1)S(1)} %fusion.3), channel_id=1, replica_groups=mesh['samp'=64,'var'=4] {'var'}, use_global_device_ids=true, to_apply=%region_0.1 | all-reduce | flops 8192 | bytes 32768 | tf_op jit(solution)/shard_map/psum | solution.py:51
  95.5 0.2 fusion.11
  95.7 1.5 convolution_subtract_fusion.2
  97.2 0.0 all-reduce.7.cloned.1.call-update
  97.2 0.0 all-reduce.9.cloned.1.call-start
  97.3 0.1 broadcast_in_dim.26
  97.4 0.1 div.40
  97.4 127.1 %psum.58 = f32[32]{0:T(128)S(1)} all-reduce(f32[32]{0:T(128)S(1)} %get-tuple-element.2), channel_id=1, replica_groups=mesh['samp'=64,'var'=4] {'samp'}, use_global_device_ids=true, to_apply=%region_4.5 | all-reduce | flops 32 | bytes 256 | tf_op jit(solution)/shard_map/psum | solution.py:24
  224.5 131.6 %all-reduce.7.cloned.1.call-done = f32[4096,32]{0,1:T(8,128)} async-done(((f32[4096,32]{0,1:T(8,128)}), f32[4096,32]{0,1:T(8,128)}) %all-reduce.7.cloned.1.call-update) | async-done | bytes 524304 | tf_op jit(solution)/shard_map/psum | solution.py:75
  356.1 1.8 convolution_bitcast_fusion.2
  357.9 0.5 fusion.4
  358.5 0.0 dynamic-slice-start
  358.5 14.0 %psum.60 = bf16[256,32]{0,1:T(8,128)(2,1)S(1)} all-reduce(bf16[256,32]{0,1:T(8,128)(2,1)S(1)} %fusion.4), channel_id=1, replica_groups=mesh['samp'=64,'var'=4] {'var'}, use_global_device_ids=true, to_apply=%region_7.8 | all-reduce | flops 8192 | bytes 32768 | tf_op jit(solution)/shard_map/psum | solution.py:51
  372.5 0.2 convert_reduce_fusion.1
  372.7 1.5 convolution_subtract_fusion.1
  374.2 0.0 all-reduce.9.cloned.1.call-update
  374.3 0.0 all-reduce.5.cloned.1.call-start
  374.3 4.6 fusion
  379.0 0.0 all-reduce.5.cloned.1.call-update
  379.0 0.0 all-reduce.11.cloned.1.call-start
  379.0 250.2 %all-reduce.9.cloned.1.call-done = f32[4096,32]{0,1:T(8,128)} async-done(((f32[4096,32]{0,1:T(8,128)}), f32[4096,32]{0,1:T(8,128)}) %all-reduce.9.cloned.1.call-update) | async-done | bytes 524304 | tf_op jit(solution)/shard_map/psum | solution.py:75
  629.3 1.6 multiply_add_fusion
  630.9 0.5 convolution_bitcast_fusion.1
  631.4 0.4 fusion.5
  631.9 0.0 dynamic-slice-start.1
  631.9 13.9 %psum.62 = bf16[256,32]{0,1:T(8,128)(2,1)S(1)} all-reduce(bf16[256,32]{0,1:T(8,128)(2,1)S(1)} %fusion.5), channel_id=1, replica_groups=mesh['samp'=64,'var'=4] {'var'}, use_global_device_ids=true, to_apply=%region_10.11 | all-reduce | flops 8192 | bytes 32768 | tf_op jit(solution)/shard_map/psum | solution.py:51
  645.8 0.2 convert_reduce_fusion
  646.0 1.5 convolution_subtract_fusion
  647.5 0.0 all-reduce.11.cloned.1.call-update
  647.5 172.9 %all-reduce.5.cloned.1.call-done = f32[10240,32]{0,1:T(8,128)} async-done(((f32[10240,32]{0,1:T(8,128)}), f32[10240,32]{0,1:T(8,128)}) %all-reduce.5.cloned.1.call-update) | async-done | bytes 1310736 | tf_op jit(solution)/shard_map/psum | solution.py:61
  820.4 2.3 fusion.2
  822.7 256.9 %all-reduce.11.cloned.1.call-done = f32[4096,32]{0,1:T(8,128)} async-done(((f32[4096,32]{0,1:T(8,128)}), f32[4096,32]{0,1:T(8,128)}) %all-reduce.11.cloned.1.call-update) | async-done | bytes 524304 | tf_op jit(solution)/shard_map/psum | solution.py:75
  1079.6 1.1 broadcast_multiply_fusion
  1080.6 0.8 minimum_subtract_fusion.1
  (32 shorter events, 0.1 us)
Async XLA Ops:
  7.2 348.9 %all-reduce.7.cloned.1.call-start = ((), (), s32[]{:S(2)}) async-start(), calls=%async_computation.1 | async-start | bytes 1048576 | tf_op jit(solution)/shard_map/psum | solution.py:75
  15.2 7.9 copy-start.10
  26.6 3.2 copy-start.1
  29.8 23.1 %copy-start = (f32[40960]{0:T(1024)S(1)}, f32[40960]{0:T(1024)}, u32[]{:S(2)}) copy-start(f32[40960]{0:T(1024)} %param.10) | copy-start | bytes 491524
  52.8 23.1 %copy-start.2 = (f32[4096,32]{0,1:T(8,128)S(1)}, f32[4096,32]{0,1:T(8,128)}, u32[]{:S(2)}) copy-start(f32[4096,32]{0,1:T(8,128)} %param.15) | copy-start | bytes 1572868
  79.7 15.8 %copy-start.4 = (s32[256]{0:T(256)S(1)}, s32[256]{0:T(256)}, u32[]{:S(2)}) copy-start(s32[256]{0:T(256)} %param.13) | copy-start | bytes 3076
  79.7 15.8 %copy-start.5 = (f32[256]{0:T(256)S(1)}, f32[256]{0:T(256)}, u32[]{:S(2)}) copy-start(f32[256]{0:T(256)} %param.12) | copy-start | bytes 3076
  80.1 17.1 %copy-start.9 = (f32[8]{0:T(128)S(1)}, f32[8]{0:T(128)}, u32[]{:S(2)}) copy-start(f32[8]{0:T(128)} %param.16) | copy-start | bytes 100
  80.2 144.4 %copy-start.6 = (f32[32]{0:T(128)S(1)}, f32[32]{0:T(128)}, u32[]{:S(2)}) copy-start(f32[32]{0:T(128)} %param.17) | copy-start | bytes 388
  95.7 128.9 %copy-start.7 = (f32[32]{0:T(128)}, f32[32]{0:T(128)S(1)}, u32[]{:S(2)}) copy-start(f32[32]{0:T(128)S(1)} %get-tuple-element.3) | copy-start | bytes 388
  97.2 532.1 %all-reduce.9.cloned.1.call-start = ((), (), s32[]{:S(2)}) async-start(), calls=%async_computation.2 | async-start | bytes 1048576 | tf_op jit(solution)/shard_map/psum | solution.py:75
  356.1 1.8 copy-start.3
  358.5 15.9 %dynamic-slice-start = ((f32[40960]{0:T(1024)}, s32[]{:T(128)}), f32[10240]{0:T(1024)S(1)}, s32[]{:S(2)}) async-start(f32[40960]{0:T(1024)} %param.10, s32[]{:T(128)} %select_n.39), calls=%async_computation.4 | async-start | bytes 82432 | tf_op jit(solution)/shard_map/dynamic_slice | solution.py:56
  358.5 15.9 %copy-start.8 = (f32[32]{0:T(128)S(1)}, f32[32]{0:T(128)}, u32[]{:S(2)}) copy-start(f32[32]{0:T(128)} %copy-done.7) | copy-start | bytes 388
  374.3 446.2 %all-reduce.5.cloned.1.call-start = ((), (), s32[]{:S(2)}) async-start(), calls=%async_computation | async-start | bytes 2621440 | tf_op jit(solution)/shard_map/psum | solution.py:61
  379.0 700.6 %all-reduce.11.cloned.1.call-start = ((), (), s32[]{:S(2)}) async-start(), calls=%async_computation.3 | async-start | bytes 1048576 | tf_op jit(solution)/shard_map/psum | solution.py:75
  631.9 188.6 %dynamic-slice-start.1 = ((f32[40960]{0:T(1024)}, s32[]{:T(128)}), f32[10240]{0:T(1024)S(1)}, s32[]{:S(2)}) async-start(f32[40960]{0:T(1024)} %param.11, s32[]{:T(128)} %select_n.39), calls=%async_computation.5 | async-start | bytes 82432 | tf_op jit(solution)/shard_map/dynamic_slice | solution.py:57
Sparse Core Ops, SparseCore 0:
  97.3 258.7 all-reduce.6
  374.4 254.8 all-reduce.8
  632.7 187.6 all-reduce.4
  825.7 253.7 all-reduce.10
where the time goes:
time: 1090 us
  waiting for transfers between devices  812 us (74%)
  blocking collectives  170 us (16%)
  local copies, waits for them, and re-layouts  68.7 us (6%)
  between operations  14 us (1%)
  matrix products  13.4 us (1%)
    psum x3, waiting for transfers between devices, shards(): gradient_total = lax.psum(gradient_cross, ('samp', 'var'))  639 us
    psum x1, waiting for transfers between devices, shards(): lax.psum(cross - local_centers[:, None] * column_sums[None, :], 'samp')  173 us
    psum x1, blocking collectives, shards(): counts = lax.psum(jnp.sum(weights, axis=0), 'samp')  127 us
    psum x3, blocking collectives, residual_of(): lax.psum(partial_fit.astype(jnp.bfloat16), 'var').astype(jnp.float32)  43.3 us
    gather x1, local copies, waits for them, and re-layouts, shards(): strong_scales = scales[columns]  23 us
    gather x1, local copies, waits for them, and re-layouts, shards(): strong_centers = centers[columns]  23 us
  transfers between devices with their start and end apart: 4, of which 4 were waited for; matrix products, arithmetic and copies ran while one was open for 1% of the time, Pallas kernels for 0%

commit v1 on v0

--- a/solution.py
+++ b/solution.py
@@ -1,3 +1,4 @@
+import functools
 import math
 import jax
 import jax.numpy as jnp
@@ -10,6 +11,15 @@
 FOLDS = 4
 ITERS = 3
 exact_mode = lax.Precision.HIGHEST
+
+
+def deliver_goods_up(incoming_x, axis_id, which_axis):
+    for i0 in (axis_id, which_axis):
+        incoming_x = lax.psum(incoming_x, i0)
+    return incoming_x
+
+
+manage_ticks_on = functools.partial(deliver_goods_up, axis_id="samp", which_axis="var")
 
 
 def shards(
@@ -72,7 +82,7 @@
             masked, rounded, (((0,), (0,)), ((), ())), preferred_element_type=jnp.float32
         )
         gradient_cross = gradient_cross - part_centers[:, None] * column_sums[None, :]
-        gradient_total = lax.psum(gradient_cross, ("samp", "var"))
+        gradient_total = manage_ticks_on(gradient_cross)
         moved = point + step_size[None, :] * (
             strong_scales[:, None] * gradient_total / counts[None, :]
         )

time: 1090 us -> 925 us (0.85)
  waiting for transfers between devices: 812 us -> 646 us
    psum x3 -> x5, waiting for transfers between devices: 639 us -> 454 us  [deliver_goods_up(): incoming_x = lax.psum(incoming_x, i0)]
    psum x1, waiting for transfers between devices: 173 us -> 192 us  [shards(): lax.psum(cross - local_centers[:, None] * column_sums[None, :], 'samp')]
  transfers between devices with their start and end apart: 4 -> 6, of which waited for: 4 -> 5; matrix products, arithmetic and copies ran while one was open for 1% -> 1% of each run, Pallas kernels for 0% -> 0%
where the time goes in v1:
time: 925 us; the launch traced here: 923 us
  waiting for transfers between devices  646 us (70%)
  blocking collectives  170 us (18%)
  local copies, waits for them, and re-layouts  68.7 us (7%)
  matrix products  14.6 us (2%)
  between operations  14.4 us (2%)
  other arithmetic  10.2 us (1%)
    psum x5, waiting for transfers between devices, deliver_goods_up(): incoming_x = lax.psum(incoming_x, i0)  454 us
    psum x1, waiting for transfers between devices, shards(): lax.psum(cross - local_centers[:, None] * column_sums[None, :], 'samp')  192 us
    psum x1, blocking collectives, shards(): counts = lax.psum(jnp.sum(weights, axis=0), 'samp')  125 us
    psum x3, blocking collectives, residual_of(): lax.psum(partial_fit.astype(jnp.bfloat16), 'var').astype(jnp.float32)  44.5 us
    gather x1, local copies, waits for them, and re-layouts, shards(): strong_scales = scales[columns]  23 us
    gather x1, local copies, waits for them, and re-layouts, shards(): strong_centers = centers[columns]  23 us
  transfers between devices with their start and end apart: 6, of which 5 were waited for; matrix products, arithmetic and copies ran while one was open for 1% of the time, Pallas kernels for 0%

profile of v1, /device:TPU:2, one launch (start us, length us, event | category | flops | bytes accessed | tf_op | source)
XLA Modules:
  0.0 923.5 jit_solution(15734939986361196987)
XLA Ops:
  7.2 0.0 all-reduce.8.cloned.1.call-start
  7.2 7.9 copy.11
  15.2 7.9 copy.12
  23.1 3.4 gather_fusion
  26.6 2.9 copy.13
  29.5 0.1 broadcast_bitcast_fusion
  29.6 0.1 broadcast_bitcast_fusion.1
  29.7 0.1 iota_add_fusion
  29.8 23.0 %gather_fusion.1 = f32[4096]{0:T(1024)S(1)} fusion(f32[40960]{0:T(1024)S(1)} %copy-done.1, s32[4096]{0:T(1024)S(1)} %broadcast_clamp_fusion), kind=kCustom, calls=%fused_computation.1 | custom fusion | bytes 49152 | tf_op jit(solution)/shard_map/gather | solution.py:48
  52.9 23.0 %gather_fusion.2 = f32[4096]{0:T(1024)S(1)} fusion(f32[40960]{0:T(1024)S(1)} %copy-done, s32[4096]{0:T(1024)S(1)} %broadcast_clamp_fusion), kind=kCustom, calls=%fused_computation.2 | custom fusion | bytes 49152 | tf_op jit(solution)/shard_map/gather | solution.py:47
  75.9 0.1 fusion.23
  76.0 0.5 convolution_bitcast_fusion.3
  76.5 3.2 fusion.1
  79.7 0.4 fusion.3
  80.2 15.3 %psum.77 = bf16[256,32]{0,1:T(8,128)(2,1)S(1)} all-reduce(bf16[256,32]{0,1:T(8,128)(2,1)S(1)} %fusion.3), channel_id=1, replica_groups=mesh['samp'=64,'var'=4] {'var'}, use_global_device_ids=true, to_apply=%region_0.1 | all-reduce | flops 8192 | bytes 32768 | tf_op jit(solution)/shard_map/psum | solution.py:61
  95.5 0.2 fusion.11
  95.7 1.5 convolution_subtract_fusion.2
  97.2 0.0 all-reduce.8.cloned.1.call-update
  97.2 0.0 all-reduce.10.cloned.1.call-start
  97.3 186.0 %all-reduce.8.cloned.1.call-done = f32[4096,32]{0,1:T(8,128)} async-done(((f32[4096,32]{0,1:T(8,128)}), f32[4096,32]{0,1:T(8,128)}) %all-reduce.8.cloned.1.call-update) | async-done | bytes 524304 | tf_op jit(solution)/shard_map/psum | solution.py:18
  283.3 0.0 all-reduce.10.cloned.1.call-update
  283.4 0.0 all-reduce.12.cloned.1.call-start
  283.4 0.1 broadcast_in_dim.26
  283.5 0.1 div.40
  283.6 125.2 %psum.79 = f32[32]{0:T(128)S(1)} all-reduce(f32[32]{0:T(128)S(1)} %get-tuple-element.2), channel_id=1, replica_groups=mesh['samp'=64,'var'=4] {'samp'}, use_global_device_ids=true, to_apply=%region_4.5 | all-reduce | flops 32 | bytes 256 | tf_op jit(solution)/shard_map/psum | solution.py:34
  408.7 0.6 fusion.22
  409.3 1.8 convolution_bitcast_fusion.2
  411.2 1.8 fusion.4
  412.9 14.7 %psum.82 = bf16[256,32]{0,1:T(8,128)(2,1)S(1)} all-reduce(bf16[256,32]{0,1:T(8,128)(2,1)} %fusion.4), channel_id=1, replica_groups=mesh['samp'=64,'var'=4] {'var'}, use_global_device_ids=true, to_apply=%region_8.9 | all-reduce | flops 8192 | bytes 32768 | tf_op jit(solution)/shard_map/psum | solution.py:61
  427.6 0.2 convert_reduce_fusion.1
  427.8 1.5 convolution_subtract_fusion.1
  429.4 0.0 all-reduce.14.cloned.1.call-start
  429.4 182.2 %all-reduce.12.cloned.1.call-done = f32[4096,32]{0,1:T(8,128)} async-done(((f32[4096,32]{0,1:T(8,128)}), f32[4096,32]{0,1:T(8,128)}) %all-reduce.12.cloned.1.call-update) | async-done | bytes 524304 | tf_op jit(solution)/shard_map/psum | solution.py:18
  611.6 0.0 all-reduce.18.cloned.1.call-start
  611.7 4.6 fusion
  616.4 41.6 %all-reduce.14.cloned.1.call-done = f32[4096,32]{0,1:T(8,128)} async-done(((f32[4096,32]{0,1:T(8,128)}), f32[4096,32]{0,1:T(8,128)}) %all-reduce.14.cloned.1.call-update) | async-done | bytes 524304 | tf_op jit(solution)/shard_map/psum | solution.py:18
  658.0 1.6 multiply_add_fusion
  659.6 0.5 convolution_bitcast_fusion.1
  660.1 0.4 fusion.5
  660.5 14.5 %psum.85 = bf16[256,32]{0,1:T(8,128)(2,1)S(1)} all-reduce(bf16[256,32]{0,1:T(8,128)(2,1)S(1)} %fusion.5), channel_id=1, replica_groups=mesh['samp'=64,'var'=4] {'var'}, use_global_device_ids=true, to_apply=%region_12.13 | all-reduce | flops 8192 | bytes 32768 | tf_op jit(solution)/shard_map/psum | solution.py:61
  675.0 0.2 convert_reduce_fusion
  675.2 1.5 convolution_subtract_fusion
  676.8 0.0 all-reduce.16.cloned.1.call-start
  676.8 191.6 %all-reduce.18.cloned.1.call-done = (f32[10240,32]{0,1:T(8,128)}, f32[4096,32]{0,1:T(8,128)}) async-done(((f32[10240,32]{0,1:T(8,128)}, f32[4096,32]{0,1:T(8,128)}), (f32[10240,32]{0,1:T(8,128)}, f32[4096,32]{0,1:T(8,128)})) %all-reduce.18.cloned.1.call-update) | async-done | bytes 1835024 | tf_op jit(solution)/shard_map/psum | solution.py:71
  868.5 2.3 fusion.2
  870.7 44.0 %all-reduce.16.cloned.1.call-done = f32[4096,32]{0,1:T(8,128)} async-done(((f32[4096,32]{0,1:T(8,128)}), f32[4096,32]{0,1:T(8,128)}) %all-reduce.16.cloned.1.call-update) | async-done | bytes 524304 | tf_op jit(solution)/shard_map/psum | solution.py:18
  914.8 1.1 broadcast_multiply_fusion
  915.8 0.8 minimum_subtract_fusion.1
  (51 shorter events, 0.2 us)
Async XLA Ops:
  7.2 276.2 %all-reduce.8.cloned.1.call-start = ((), (), s32[]{:S(2)}) async-start(), calls=%async_computation | async-start | bytes 1048576 | tf_op jit(solution)/shard_map/psum | solution.py:18
  15.2 7.9 copy-start.17
  26.6 3.2 copy-start.1
  29.8 23.1 %copy-start = (f32[40960]{0:T(1024)S(1)}, f32[40960]{0:T(1024)}, u32[]{:S(2)}) copy-start(f32[40960]{0:T(1024)} %param.10) | copy-start | bytes 491524
  52.8 23.1 %copy-start.2 = (f32[4096,32]{0,1:T(8,128)S(1)}, f32[4096,32]{0,1:T(8,128)}, u32[]{:S(2)}) copy-start(f32[4096,32]{0,1:T(8,128)} %param.15) | copy-start | bytes 1572868
  79.7 15.8 %copy-start.4 = (s32[256]{0:T(256)S(1)}, s32[256]{0:T(256)}, u32[]{:S(2)}) copy-start(s32[256]{0:T(256)} %param.13) | copy-start | bytes 3076
  79.7 15.8 %copy-start.5 = (f32[256]{0:T(256)S(1)}, f32[256]{0:T(256)}, u32[]{:S(2)}) copy-start(f32[256]{0:T(256)} %param.12) | copy-start | bytes 3076
  80.1 203.3 %copy-start.16 = (f32[8]{0:T(128)S(1)}, f32[8]{0:T(128)}, u32[]{:S(2)}) copy-start(f32[8]{0:T(128)} %param.16) | copy-start | bytes 100
  80.2 328.6 %copy-start.6 = (f32[32]{0:T(128)S(1)}, f32[32]{0:T(128)}, u32[]{:S(2)}) copy-start(f32[32]{0:T(128)} %param.17) | copy-start | bytes 388
  95.7 187.7 %copy-start.14 = (f32[32]{0:T(128)}, f32[32]{0:T(128)S(1)}, u32[]{:S(2)}) copy-start(f32[32]{0:T(128)S(1)} %get-tuple-element.3) | copy-start | bytes 388
  97.2 312.1 %all-reduce.10.cloned.1.call-start = ((), (), s32[]{:S(2)}) async-start(), calls=%async_computation.1 | async-start | bytes 1048576 | tf_op jit(solution)/shard_map/psum | solution.py:18
  283.4 328.3 %all-reduce.12.cloned.1.call-start = ((), (), s32[]{:S(2)}) async-start(), calls=%async_computation.2 | async-start | bytes 1048576 | tf_op jit(solution)/shard_map/psum | solution.py:18
  283.6 125.7 %copy-start.12 = (f32[32]{0:T(128)}, f32[32]{0:T(128)S(1)}, u32[]{:S(2)}) copy-start(f32[32]{0:T(128)S(1)} %div.40) | copy-start | bytes 388
  409.3 1.8 copy-start.3
  409.3 1.8 copy-start.8
  409.3 1.8 copy-start.10
  412.9 198.8 %copy-start.15 = (f32[32]{0:T(128)S(1)}, f32[32]{0:T(128)}, u32[]{:S(2)}) copy-start(f32[32]{0:T(128)} %copy-done.14) | copy-start | bytes 388
  429.4 228.6 %all-reduce.14.cloned.1.call-start = ((), (), s32[]{:S(2)}) async-start(), calls=%async_computation.3 | async-start | bytes 1048576 | tf_op jit(solution)/shard_map/psum | solution.py:18
  611.6 256.8 %all-reduce.18.cloned.1.call-start = ((), (), s32[]{:S(2)}) async-start(), calls=%async_computation.5 | async-start | bytes 3670016 | tf_op jit(solution)/shard_map/psum | solution.py:71
  611.7 46.3 %copy-start.7 = (f32[32]{0:T(128)S(1)}, f32[32]{0:T(128)}, u32[]{:S(2)}) copy-start(f32[32]{0:T(128)} %param.17) | copy-start | bytes 388
  611.7 46.2 %copy-start.9 = (f32[32]{0:T(128)S(1)}, f32[32]{0:T(128)}, u32[]{:S(2)}) copy-start(f32[32]{0:T(128)} %get-tuple-element.6) | copy-start | bytes 388
  611.7 46.2 %copy-start.11 = (f32[32]{0:T(128)S(1)}, f32[32]{0:T(128)}, u32[]{:S(2)}) copy-start(f32[32]{0:T(128)} %get-tuple-element.7) | copy-start | bytes 388
  675.2 193.3 %dynamic-slice-start = ((f32[40960]{0:T(1024)}, s32[]{:T(128)}), f32[10240]{0:T(1024)S(1)}, s32[]{:S(2)}) async-start(f32[40960]{0:T(1024)} %param.11, s32[]{:T(128)} %select_n.39), calls=%async_computation.6 | async-start | bytes 82432 | tf_op jit(solution)/shard_map/dynamic_slice | solution.py:67
  675.2 193.3 %copy-start.13 = (f32[32]{0:T(128)S(1)}, f32[32]{0:T(128)}, u32[]{:S(2)}) copy-start(f32[32]{0:T(128)} %copy-done.12) | copy-start | bytes 388
  676.8 238.0 %all-reduce.16.cloned.1.call-start = ((), (), s32[]{:S(2)}) async-start(), calls=%async_computation.4 | async-start | bytes 1048576 | tf_op jit(solution)/shard_map/psum | solution.py:18
Sparse Core Ops, SparseCore 0:
  97.4 185.9 all-reduce.7
  285.7 44.2 all-reduce.9
  429.5 182.0 all-reduce.11
  613.8 44.1 all-reduce.13
  676.9 191.5 all-reduce.17
  870.6 44.0 all-reduce.15
